TPU v7x, 32 devices: a whole 2x2x4 slice. The times are simulated.
32 devices in a mesh: grp: 2 (over x), row: 16 (over z, y, core).
Axes of the slice: x: 2, y: 2, z: 4, core: 2. Of those that a mesh axis runs over, the one named last changes fastest.
Arguments:
- greens: bfloat16 [8192, 16384], P(('grp', 'row')), parts along dimension 0, may hold values from -0.0625 to 0.0625
- track_id: int32 [8192], P(('grp', 'row')), parts along dimension 0, may hold values from 0 to 7
- sigma_inv: float32 [16], P('grp'), parts along dimension 0, may hold values from 1 to 10
- sketch: float32 [192, 128, 128], P('grp', 'row'), parts along dimension 0, may hold values from -6 to 6
Outputs:
- range_basis: float32 [8192, 96], P(('grp', 'row')), parts along dimension 0
- coefficients: float32 [256, 128, 96], P(('grp', 'row')), parts along dimension 0
There are 2 independent parts, one for each index of `grp`. A program takes and returns all parts, laid end to end along the dimension named above; each array names one. Nothing has to cross between parts.
All inputs are finite; a program needn't handle non-finite values.
Results may differ from a plain program's by a relative error of at most 0.011.
Values may be sent and summed in bfloat16 or wider, within the bound.
No kernel may reach another device: no remote copies, remote signals or barrier semaphores. Data moves between devices by JAX's collectives and lax.ppermute only.
A program may use at most 128 MiB of HBM per device.

v0:
```python
import jax
import jax.numpy as jnp
from jax import lax
from jax.sharding import PartitionSpec as P

SWEEPS = 4
smoothing = 0.24


def with_halo(x, sides, width):
    for axis, dim in sides:
        count, length = (lax.axis_size(axis), x.shape[dim])
        up = [(i, (i + 1) % count) for i in range(count - 1)]
        down = [(j, i) for i, j in up]
        last = lax.slice_in_dim(x, length - width, length, axis=dim)
        initial = lax.slice_in_dim(x, 0, width, axis=dim)
        before = lax.ppermute(last, axis, up)
        after = lax.ppermute(initial, axis, down)
        x = jnp.concatenate([before, x, after], axis=dim)
    return x


def smooth_padded(padded, field):
    padded = jnp.pad(padded, ((0, 0), (0, 0), (1, 1)))
    beside_all = (
        padded[:, 2:, 1:-1] + padded[:, :-2, 1:-1] + padded[:, 1:-1, 2:] + padded[:, 1:-1, :-2]
    )
    return field + smoothing * (beside_all - 4.0 * field)


def orthonormalize(sketched, total_rows):
    local_gram = jnp.dot(sketched.T, sketched, precision=lax.Precision.HIGHEST)
    gram_matrix = lax.psum(local_gram, "row") / total_rows
    factor = jnp.linalg.cholesky(gram_matrix)
    return lax.linalg.triangular_solve(
        factor, sketched, left_side=False, lower=True, transpose_a=True
    )


def local(greens, track_id, sigma_inv, sketch):
    local_rows = greens.shape[0]
    columns_count = sketch.shape[0]
    total_rows = local_rows * lax.axis_size("row")
    row_scale = 1.0 / jnp.sqrt(jnp.float32(total_rows))
    groups = jnp.arange(sigma_inv.shape[0], dtype=jnp.int32)
    onehot = (track_id[:, None] == groups[None, :]).astype(jnp.float32)
    weights = jnp.dot(onehot, sigma_inv, precision=lax.Precision.HIGHEST)
    field = sketch
    for sweep_index in range(SWEEPS):
        padded = with_halo(field, (("row", 1),), 1)
        field = smooth_padded(padded, field)
    omega = field.astype(jnp.bfloat16)
    portion = lax.all_gather(omega, "row", axis=1, tiled=True)
    strike = portion.shape[2]
    width = portion.shape[1] * strike
    columns = greens
    flattened = portion.reshape(portion.shape[0], width)
    first = lax.dot_general(
        columns, flattened, (((1,), (1,)), ((), ())), preferred_element_type=jnp.float32
    )
    basis_one = orthonormalize(first * weights[:, None], total_rows)
    weighted_one = (basis_one * weights[:, None]).astype(jnp.bfloat16)
    columns = greens
    back_local = lax.psum_scatter(
        lax.dot_general(
            columns, weighted_one, (((0,), (0,)), ((), ())), preferred_element_type=jnp.float32
        ),
        "row",
        scatter_dimension=0,
        tiled=True,
    )
    back_local = (back_local * row_scale).astype(jnp.bfloat16)
    columns = greens
    second = jnp.dot(
        columns,
        lax.all_gather(back_local, "row", axis=0, tiled=True),
        preferred_element_type=jnp.float32,
    )
    range_basis = orthonormalize(second * weights[:, None], total_rows)
    weighted_two = (range_basis * weights[:, None]).astype(jnp.bfloat16)
    columns = greens
    projected = lax.psum_scatter(
        lax.dot_general(
            columns, weighted_two, (((0,), (0,)), ((), ())), preferred_element_type=jnp.float32
        ),
        "row",
        scatter_dimension=0,
        tiled=True,
    )
    coefficients = (projected * row_scale).reshape(sketch.shape[1], sketch.shape[2], columns_count)
    return (range_basis, coefficients)


def solution(mesh):
    in_specs = (P(("grp", "row"), None), P(("grp", "row")), P("grp"), P("grp", "row", None))
    out_specs = (P(("grp", "row"), None), P(("grp", "row"), None, None))
    return jax.shard_map(local, mesh=mesh, in_specs=in_specs, out_specs=out_specs, check_vma=False)
```

profile of v0, /device:TPU:0, one launch (start us, length us, event | category | flops | bytes accessed | tf_op | source)
XLA Modules:
  0.0 502.3 jit_solution(15993353237637454936)
XLA Ops:
  7.2 0.0 copy-start
  7.2 0.0 copy-start.1
  7.2 0.0 all-gather.3.cloned.1.call-start
  7.2 1.2 fusion.43
  8.5 2.4 collective-permute-start.1
  10.9 1.3 collective-permute-start
  12.2 3.9 collective-permute-done
  16.1 1.9 select_maximum_fusion.6
  18.0 0.3 fusion.24
  18.3 0.1 fusion.42
  18.4 4.7 collective-permute-start.3
  23.1 1.3 collective-permute-start.2
  24.4 0.0 collective-permute-done.3
  24.4 1.8 collective-permute-done.2
  26.2 0.9 select_maximum_fusion.4
  27.1 0.3 fusion.20
  27.4 0.1 fusion.41
  27.5 5.0 collective-permute-start.5
  32.5 1.3 collective-permute-start.4
  33.8 1.8 collective-permute-done.4
  35.6 0.9 select_maximum_fusion.2
  36.5 0.3 fusion.16
  36.8 0.1 fusion.40
  36.9 5.1 %collective-permute-start.7 = (f32[96,1,128]{2,1,0:T(1,128)S(1)}, f32[96,1,128]{2,1,0:T(1,128)S(1)}, u32[]{:S(2)}, u32[]{:S(2)}) collective-permute-start(f32[96,1,128]{2,1,0:T(1,128)S(1)} %get-tuple-element.6), channel_id=1, source_target_pairs={{0,1},{1,2},{2,3},{3,4},{4,5},{5,6},{6,7},{7,8},{8,9},{9,10},{10,1... | collective-permute-start | bytes 147464 | tf_op jit(solution)/shard_map/ppermute | solution.py:17
  42.0 0.0 copy-start.3
  42.0 1.3 collective-permute-start.6
  43.3 1.8 collective-permute-done.6
  45.2 0.9 select_maximum_fusion
  46.1 1.0 fusion.12
  47.1 0.0 all-gather.3.cloned.1.call-update
  47.1 0.0 reduce-scatter.3.cloned.1.call-start
  47.2 0.2 fusion.26
  47.3 50.3 %all-gather.3.cloned.1.call-done = bf16[96,128,128]{2,1,0:T(8,128)(2,1)} async-done(((bf16[96,8,128]{2,1,0:T(8,128)(2,1)}), bf16[96,128,128]{2,1,0:T(8,128)(2,1)}) %all-gather.3.cloned.1.call-update) | async-done | bytes 3145744 | tf_op jit(solution)/shard_map/all_gather | solution.py:53
  97.6 7.7 %fusion.5 = f32[96,256]{1,0:T(8,128)S(1)} fusion(bf16[256,16384]{1,0:T(8,128)(2,1)} %param.7, bf16[12,8,128,128]{3,2,1,0:T(8,128)(2,1)} %bitcast.61, f32[256]{0:T(256)S(1)} %bitcast.62), kind=kOutput, calls=%fused_computation.20 | convolution fusion | flops 805330944 | bytes 11633664 | tf_op jit(solution)/shard_map/dot_general | solution.py:58
  105.4 0.2 fusion.44
  105.6 58.9 %psum.14 = f32[96,96]{0,1:T(8,128)S(1)} all-reduce(f32[96,96]{0,1:T(8,128)S(1)} %fusion.44), channel_id=1, replica_groups=mesh['grp'=2,'row'=16] {'row'}, use_global_device_ids=true, to_apply=%region_0.1 | all-reduce | flops 9216 | bytes 73728 | tf_op jit(solution)/shard_map/psum | solution.py:33
  164.5 0.1 copy.7
  164.6 8.8 %cholesky.44 = f32[96,96]{1,0:T(8,128)S(1)} custom-call(f32[96,96]{1,0:T(8,128)S(1)} %fusion.35), custom_call_target="Cholesky" | custom-call | tf_op jit(solution)/shard_map/jit(cholesky)/cholesky | solution.py:34
  173.4 0.6 compare_reduce_fusion.1
  174.1 0.7 fusion.30
  174.7 7.4 %custom-call.6 = f32[1,96,96]{1,2,0:T(8,128)S(1)} custom-call(f32[1,96,96]{2,1,0:T(8,128)S(1)} %fusion.30), custom_call_target="InvertDiagBlocksLowerTriangular" | custom-call | tf_op jit(solution)/shard_map/triangular_solve/custom-call.0 | solution.py:35
  182.1 0.3 fusion.8
  182.4 7.5 %convolution_bitcast_fusion.1 = f32[16384,96]{0,1:T(8,128)} fusion(bf16[256,96]{0,1:T(8,128)(2,1)S(1)} %fusion.8, bf16[256,16384]{1,0:T(8,128)(2,1)} %param.7), kind=kOutput, calls=%fused_computation.1 | convolution fusion | flops 805306368 | bytes 14729216 | tf_op jit(solution)/shard_map/dot_general | solution.py:65
  189.9 0.0 reduce-scatter.3.cloned.1.call-update
  189.9 0.0 all-gather.5.cloned.1.call-start
  190.0 82.4 %reduce-scatter.3.cloned.1.call-done = f32[1024,96]{0,1:T(8,128)} async-done(((f32[16384,96]{0,1:T(8,128)}), f32[1024,96]{0,1:T(8,128)}) %reduce-scatter.3.cloned.1.call-update) | async-done | bytes 393232 | tf_op jit(solution)/shard_map/reduce_scatter | solution.py:64
  272.3 1.7 multiply_convert_fusion
  274.0 0.0 all-gather.5.cloned.1.call-update
  274.1 0.0 reduce-scatter.5.cloned.1.call-start
  274.1 45.6 %all-gather.5.cloned.1.call-done = bf16[16384,96]{0,1:T(8,128)(2,1)} async-done(((bf16[1024,96]{0,1:T(8,128)(2,1)}), bf16[16384,96]{0,1:T(8,128)(2,1)}) %all-gather.5.cloned.1.call-update) | async-done | bytes 3145744 | tf_op jit(solution)/shard_map/all_gather | solution.py:76
  319.7 7.1 %convolution_multiply_fusion = f32[96,256]{1,0:T(8,128)S(1)} fusion(bf16[16384,96]{0,1:T(8,128)(2,1)} %all-gather.5.cloned.1.call-done, bf16[256,16384]{1,0:T(8,128)(2,1)} %param.7, f32[256]{0:T(256)S(1)} %bitcast.64), kind=kOutput, calls=%fused_computation.17 | convolution fusion | flops 805330944 | bytes 11633664 | tf_op jit(solution)/shard_map/dot_general | solution.py:74
  326.8 0.2 fusion.45
  327.0 59.1 %psum.15 = f32[96,96]{0,1:T(8,128)S(1)} all-reduce(f32[96,96]{0,1:T(8,128)S(1)} %fusion.45), channel_id=1, replica_groups=mesh['grp'=2,'row'=16] {'row'}, use_global_device_ids=true, to_apply=%region_4.7 | all-reduce | flops 9216 | bytes 73728 | tf_op jit(solution)/shard_map/psum | solution.py:33
  386.2 0.1 copy.9
  386.3 8.8 %cholesky.55 = f32[96,96]{1,0:T(8,128)S(1)} custom-call(f32[96,96]{1,0:T(8,128)S(1)} %fusion.33), custom_call_target="Cholesky" | custom-call | tf_op jit(solution)/shard_map/jit(cholesky)/cholesky | solution.py:34
  395.1 0.6 compare_reduce_fusion
  395.7 0.7 fusion.31
  396.4 7.4 %custom-call.7 = f32[1,96,96]{1,2,0:T(8,128)S(1)} custom-call(f32[1,96,96]{2,1,0:T(8,128)S(1)} %fusion.31), custom_call_target="InvertDiagBlocksLowerTriangular" | custom-call | tf_op jit(solution)/shard_map/triangular_solve/custom-call.0 | solution.py:35
  403.7 0.3 convolution_bitcast_fusion.2
  404.0 0.0 copy-start.2
  404.0 7.5 %convolution_bitcast_fusion = f32[16384,96]{0,1:T(8,128)} fusion(bf16[256,16384]{1,0:T(8,128)(2,1)} %param.7, f32[256,96]{0,1:T(8,128)S(1)} %convolution_bitcast_fusion.2, f32[256]{0:T(256)S(1)} %bitcast.65), kind=kOutput, calls=%fused_computation | convolution fusion | flops 805355520 | bytes 14779392 | tf_op jit(solution)/shard_map/dot_general | solution.py:83
  411.6 0.0 reduce-scatter.5.cloned.1.call-update
  411.6 82.4 %reduce-scatter.5.cloned.1.call-done = f32[1024,96]{0,1:T(8,128)} async-done(((f32[16384,96]{0,1:T(8,128)}), f32[1024,96]{0,1:T(8,128)}) %reduce-scatter.5.cloned.1.call-update) | async-done | bytes 393232 | tf_op jit(solution)/shard_map/reduce_scatter | solution.py:82
  494.0 1.8 copy_bitcast_fusion
  (13 shorter events, 0.1 us)
Async XLA Ops:
  7.2 40.0 %copy-start = (f32[8]{0:T(128)S(1)}, f32[8]{0:T(128)}, u32[]{:S(2)}) copy-start(f32[8]{0:T(128)} %param.9) | copy-start | bytes 100
  7.2 10.8 %copy-start.1 = (f32[96,8,128]{2,1,0:T(8,128)S(1)}, f32[96,8,128]{2,1,0:T(8,128)}, u32[]{:S(2)}) copy-start(f32[96,8,128]{2,1,0:T(8,128)} %param.10) | copy-start | bytes 1179652
  7.2 90.5 %all-gather.3.cloned.1.call-start = ((), (), s32[]{:S(2)}) async-start(), calls=%async_computation.2 | async-start | bytes 3342336 | tf_op jit(solution)/shard_map/all_gather | solution.py:53
  8.5 3.7 collective-permute-start.1
  10.9 5.2 %collective-permute-start = (f32[96,1,128]{2,1,0:T(1,128)S(1)}, f32[96,1,128]{2,1,0:T(1,128)S(1)}, u32[]{:S(2)}, u32[]{:S(2)}) collective-permute-start(f32[96,1,128]{2,1,0:T(1,128)S(1)} %get-tuple-element.13), channel_id=1, source_target_pairs={{1,0},{2,1},{3,2},{4,3},{5,4},{6,5},{7,6},{8,7},{9,8},{10,9},{11,1... | collective-permute-start | bytes 147464 | tf_op jit(solution)/shard_map/ppermute | solution.py:18
  18.4 6.0 %collective-permute-start.3 = (f32[96,1,128]{2,1,0:T(1,128)S(1)}, f32[96,1,128]{2,1,0:T(1,128)S(1)}, u32[]{:S(2)}, u32[]{:S(2)}) collective-permute-start(f32[96,1,128]{2,1,0:T(1,128)S(1)} %get-tuple-element.10), channel_id=1, source_target_pairs={{0,1},{1,2},{2,3},{3,4},{4,5},{5,6},{6,7},{7,8},{8,9},{9,10},{10,1... | collective-permute-start | bytes 147464 | tf_op jit(solution)/shard_map/ppermute | solution.py:17
  23.1 3.1 collective-permute-start.2
  27.5 6.3 %collective-permute-start.5 = (f32[96,1,128]{2,1,0:T(1,128)S(1)}, f32[96,1,128]{2,1,0:T(1,128)S(1)}, u32[]{:S(2)}, u32[]{:S(2)}) collective-permute-start(f32[96,1,128]{2,1,0:T(1,128)S(1)} %get-tuple-element.8), channel_id=1, source_target_pairs={{0,1},{1,2},{2,3},{3,4},{4,5},{5,6},{6,7},{7,8},{8,9},{9,10},{10,1... | collective-permute-start | bytes 147464 | tf_op jit(solution)/shard_map/ppermute | solution.py:17
  32.5 3.1 collective-permute-start.4
  36.9 6.4 %collective-permute-start.7 = (f32[96,1,128]{2,1,0:T(1,128)S(1)}, f32[96,1,128]{2,1,0:T(1,128)S(1)}, u32[]{:S(2)}, u32[]{:S(2)}) collective-permute-start(f32[96,1,128]{2,1,0:T(1,128)S(1)} %get-tuple-element.6), channel_id=1, source_target_pairs={{0,1},{1,2},{2,3},{3,4},{4,5},{5,6},{6,7},{7,8},{8,9},{9,10},{10,1... | collective-permute-start | bytes 147464 | tf_op jit(solution)/shard_map/ppermute | solution.py:17
  42.0 5.1 %copy-start.3 = (s32[256]{0:T(256)S(1)}, s32[256]{0:T(256)}, u32[]{:S(2)}) copy-start(s32[256]{0:T(256)} %param.8) | copy-start | bytes 3076
  42.0 3.1 collective-permute-start.6
  47.1 225.3 %reduce-scatter.3.cloned.1.call-start = ((), (), s32[]{:S(2)}) async-start(), calls=%async_computation.3 | async-start | bytes 6684672 | tf_op jit(solution)/shard_map/reduce_scatter | solution.py:64
  189.9 129.8 %all-gather.5.cloned.1.call-start = ((), (), s32[]{:S(2)}) async-start(), calls=%async_computation.4 | async-start | bytes 3342336 | tf_op jit(solution)/shard_map/all_gather | solution.py:76
  274.1 219.9 %reduce-scatter.5.cloned.1.call-start = ((), (), s32[]{:S(2)}) async-start(), calls=%async_computation.5 | async-start | bytes 6684672 | tf_op jit(solution)/shard_map/reduce_scatter | solution.py:82
  404.0 7.5 %copy-start.2 = (f32[256,96]{0,1:T(8,128)}, f32[256,96]{0,1:T(8,128)S(1)}, u32[]{:S(2)}) copy-start(f32[256,96]{0,1:T(8,128)S(1)} %convolution_bitcast_fusion.2) | copy-start | bytes 294916
Sparse Core Ops, SparseCore 0:
  47.2 50.3 all-gather.2
  190.0 82.2 reduce-scatter.2
  275.1 44.5 all-gather.4
  411.7 82.2 reduce-scatter.4
where the time goes:
time: 503 us; the launch traced here: 502 us
  waiting for transfers between devices  270 us (54%)
  blocking collectives  118 us (23%)
  other arithmetic  44.9 us (9%)
  matrix products  31.1 us (6%)
  starting transfers between devices  22.5 us (4%)
  between operations  14.1 us (3%)
    psum x2, blocking collectives, orthonormalize(): gram_matrix = lax.psum(local_gram, 'row') / total_rows  118 us
    reduce_scatter x1, waiting for transfers between devices, local(): lax.psum_scatter(lax.dot_general(columns, weighted_one, (((0,), (0,)), ((...  82.4 us
    reduce_scatter x1, waiting for transfers between devices, local(): lax.psum_scatter(lax.dot_general(columns, weighted_two, (((0,), (0,)), ((...  82.4 us
    all_gather x1, waiting for transfers between devices, local(): portion = lax.all_gather(omega, 'row', axis=1, tiled=True)  50.3 us
    all_gather x1, waiting for transfers between devices, local(): lax.all_gather(back_local, 'row', axis=0, tiled=True)  45.6 us
    another operation x6, other arithmetic, orthonormalize(): factor = jnp.linalg.cholesky(gram_matrix)  18.9 us
    ppermute x4, starting transfers between devices, with_halo(): before = lax.ppermute(last, axis, up)  17.2 us
    another operation x4, other arithmetic, orthonormalize(): lax.linalg.triangular_solve(factor, sketched, left_side=False, lower=True...  16 us
  transfers between devices with their start and end apart: 12, of which 8 were waited for; matrix products, arithmetic and copies ran while one was open for 0% of the time, Pallas kernels for 0%

commit v1 on v0

--- a/solution.py
+++ b/solution.py
@@ -30,7 +30,7 @@
 
 def orthonormalize(sketched, total_rows):
     local_gram = jnp.dot(sketched.T, sketched, precision=lax.Precision.HIGHEST)
-    gram_matrix = lax.psum(local_gram, "row") / total_rows
+    gram_matrix = jnp.sum(lax.all_gather(local_gram, "row"), axis=0) / total_rows
     factor = jnp.linalg.cholesky(gram_matrix)
     return lax.linalg.triangular_solve(
         factor, sketched, left_side=False, lower=True, transpose_a=True

time: 503 us -> 427 us (0.85)
  blocking collectives: 118 us -> 42.1 us
    psum x2 -> x0, blocking collectives: 118 us -> none  [orthonormalize(): gram_matrix = lax.psum(local_gram, 'row') / total_rows]
    all_gather x0 -> x2, blocking collectives: none -> 42.1 us  [orthonormalize(): lax.all_gather(local_gram, 'row')]
where the time goes in v1:
time: 427 us
  waiting for transfers between devices  270 us (63%)
  other arithmetic  45 us (11%)
  blocking collectives  42.1 us (10%)
  matrix products  31.1 us (7%)
  starting transfers between devices  22.5 us (5%)
  between operations  14.1 us (3%)
    reduce_scatter x1, waiting for transfers between devices, local(): lax.psum_scatter(lax.dot_general(columns, weighted_one, (((0,), (0,)), ((...  82.4 us
    reduce_scatter x1, waiting for transfers between devices, local(): lax.psum_scatter(lax.dot_general(columns, weighted_two, (((0,), (0,)), ((...  82.4 us
    all_gather x1, waiting for transfers between devices, local(): portion = lax.all_gather(omega, 'row', axis=1, tiled=True)  50.3 us
    all_gather x1, waiting for transfers between devices, local(): lax.all_gather(back_local, 'row', axis=0, tiled=True)  45.7 us
    all_gather x2, blocking collectives, orthonormalize(): lax.all_gather(local_gram, 'row')  42.1 us
    another operation x6, other arithmetic, orthonormalize(): factor = jnp.linalg.cholesky(gram_matrix)  18.9 us
    ppermute x4, starting transfers between devices, with_halo(): before = lax.ppermute(last, axis, up)  17.2 us
    another operation x4, other arithmetic, orthonormalize(): lax.linalg.triangular_solve(factor, sketched, left_side=False, lower=True...  16 us
  transfers between devices with their start and end apart: 12, of which 8 were waited for; matrix products, arithmetic and copies ran while one was open for 0% of the time, Pallas kernels for 0%

profile of v1, /device:TPU:0, one launch (start us, length us, event | category | flops | bytes accessed | tf_op | source)
XLA Modules:
  0.0 426.8 jit_solution(1737643794299798763)
XLA Ops:
  7.2 0.0 copy-start
  7.2 0.0 all-gather.5.cloned.1.call-start
  7.2 1.2 fusion.43
  8.5 2.4 collective-permute-start.1
  10.9 1.3 collective-permute-start
  12.2 3.9 collective-permute-done
  16.1 1.9 select_maximum_fusion.6
  18.0 0.3 fusion.24
  18.3 0.1 fusion.42
  18.4 4.7 %collective-permute-start.3 = (f32[96,1,128]{2,1,0:T(1,128)S(1)}, f32[96,1,128]{2,1,0:T(1,128)S(1)}, u32[]{:S(2)}, u32[]{:S(2)}) collective-permute-start(f32[96,1,128]{2,1,0:T(1,128)S(1)} %get-tuple-element.12), channel_id=1, source_target_pairs={{0,1},{1,2},{2,3},{3,4},{4,5},{5,6},{6,7},{7,8},{8,9},{9,10},{10,1... | collective-permute-start | bytes 147464 | tf_op jit(solution)/shard_map/ppermute | solution.py:17
  23.1 1.3 collective-permute-start.2
  24.4 1.8 collective-permute-done.2
  26.2 0.9 select_maximum_fusion.4
  27.1 0.3 fusion.20
  27.4 0.1 fusion.41
  27.5 5.0 %collective-permute-start.5 = (f32[96,1,128]{2,1,0:T(1,128)S(1)}, f32[96,1,128]{2,1,0:T(1,128)S(1)}, u32[]{:S(2)}, u32[]{:S(2)}) collective-permute-start(f32[96,1,128]{2,1,0:T(1,128)S(1)} %get-tuple-element.10), channel_id=1, source_target_pairs={{0,1},{1,2},{2,3},{3,4},{4,5},{5,6},{6,7},{7,8},{8,9},{9,10},{10,1... | collective-permute-start | bytes 147464 | tf_op jit(solution)/shard_map/ppermute | solution.py:17
  32.5 1.3 collective-permute-start.4
  33.8 1.8 collective-permute-done.4
  35.6 0.9 select_maximum_fusion.2
  36.5 0.3 fusion.16
  36.8 0.1 fusion.40
  36.9 5.1 %collective-permute-start.7 = (f32[96,1,128]{2,1,0:T(1,128)S(1)}, f32[96,1,128]{2,1,0:T(1,128)S(1)}, u32[]{:S(2)}, u32[]{:S(2)}) collective-permute-start(f32[96,1,128]{2,1,0:T(1,128)S(1)} %get-tuple-element.8), channel_id=1, source_target_pairs={{0,1},{1,2},{2,3},{3,4},{4,5},{5,6},{6,7},{7,8},{8,9},{9,10},{10,1... | collective-permute-start | bytes 147464 | tf_op jit(solution)/shard_map/ppermute | solution.py:17
  42.0 1.3 collective-permute-start.6
  43.3 1.8 collective-permute-done.6
  45.2 0.9 select_maximum_fusion
  46.1 1.0 fusion.12
  47.1 0.0 all-gather.5.cloned.1.call-update
  47.1 0.0 reduce-scatter.3.cloned.1.call-start
  47.2 0.2 fusion.26
  47.3 50.3 %all-gather.5.cloned.1.call-done = bf16[96,128,128]{2,1,0:T(8,128)(2,1)} async-done(((bf16[96,8,128]{2,1,0:T(8,128)(2,1)}), bf16[96,128,128]{2,1,0:T(8,128)(2,1)}) %all-gather.5.cloned.1.call-update) | async-done | bytes 3145744 | tf_op jit(solution)/shard_map/all_gather | solution.py:53
  97.6 7.7 %fusion.5 = f32[96,256]{1,0:T(8,128)S(1)} fusion(bf16[256,16384]{1,0:T(8,128)(2,1)} %param.7, bf16[12,8,128,128]{3,2,1,0:T(8,128)(2,1)} %bitcast.65, f32[256]{0:T(256)S(1)} %bitcast.66), kind=kOutput, calls=%fused_computation.20 | convolution fusion | flops 805330944 | bytes 11633664 | tf_op jit(solution)/shard_map/dot_general | solution.py:58
  105.4 0.2 fusion.44
  105.6 20.9 %all-gather = f32[1536,96]{1,0:T(8,128)S(1)} all-gather(f32[96,96]{1,0:T(8,128)S(1)} %fusion.44), channel_id=2, replica_groups=mesh['grp'=2,'row'=16] {'row'}, dimensions={0}, use_global_device_ids=true | all-gather | bytes 626688 | tf_op jit(solution)/shard_map/all_gather | solution.py:33
  126.5 0.1 reduce_sum.18
  126.5 0.1 copy.9
  126.6 0.1 copy.10
  126.7 8.8 %cholesky.44 = f32[96,96]{1,0:T(8,128)S(1)} custom-call(f32[96,96]{1,0:T(8,128)S(1)} %fusion.35), custom_call_target="Cholesky" | custom-call | tf_op jit(solution)/shard_map/jit(cholesky)/cholesky | solution.py:34
  135.6 0.6 compare_reduce_fusion.1
  136.2 0.7 fusion.30
  136.9 7.4 %custom-call.6 = f32[1,96,96]{1,2,0:T(8,128)S(1)} custom-call(f32[1,96,96]{2,1,0:T(8,128)S(1)} %fusion.30), custom_call_target="InvertDiagBlocksLowerTriangular" | custom-call | tf_op jit(solution)/shard_map/triangular_solve/custom-call.0 | solution.py:35
  144.2 0.3 fusion.8
  144.5 7.5 %convolution_bitcast_fusion.1 = f32[16384,96]{0,1:T(8,128)} fusion(bf16[256,96]{0,1:T(8,128)(2,1)S(1)} %fusion.8, bf16[256,16384]{1,0:T(8,128)(2,1)} %param.7), kind=kOutput, calls=%fused_computation.1 | convolution fusion | flops 805306368 | bytes 14729216 | tf_op jit(solution)/shard_map/dot_general | solution.py:65
  152.0 0.0 reduce-scatter.3.cloned.1.call-update
  152.0 0.0 all-gather.7.cloned.1.call-start
  152.1 82.4 %reduce-scatter.3.cloned.1.call-done = f32[1024,96]{0,1:T(8,128)} async-done(((f32[16384,96]{0,1:T(8,128)}), f32[1024,96]{0,1:T(8,128)}) %reduce-scatter.3.cloned.1.call-update) | async-done | bytes 393232 | tf_op jit(solution)/shard_map/reduce_scatter | solution.py:64
  234.5 1.7 multiply_convert_fusion
  236.2 0.0 all-gather.7.cloned.1.call-update
  236.2 0.0 reduce-scatter.5.cloned.1.call-start
  236.3 45.7 %all-gather.7.cloned.1.call-done = bf16[16384,96]{0,1:T(8,128)(2,1)} async-done(((bf16[1024,96]{0,1:T(8,128)(2,1)}), bf16[16384,96]{0,1:T(8,128)(2,1)}) %all-gather.7.cloned.1.call-update) | async-done | bytes 3145744 | tf_op jit(solution)/shard_map/all_gather | solution.py:76
  281.9 7.0 %convolution_multiply_fusion = f32[96,256]{1,0:T(8,128)S(1)} fusion(bf16[16384,96]{0,1:T(8,128)(2,1)} %all-gather.7.cloned.1.call-done, bf16[256,16384]{1,0:T(8,128)(2,1)} %param.7, f32[256]{0:T(256)S(1)} %bitcast.68), kind=kOutput, calls=%fused_computation.17 | convolution fusion | flops 805330944 | bytes 11633664 | tf_op jit(solution)/shard_map/dot_general | solution.py:74
  289.0 0.2 fusion.45
  289.2 21.2 %all-gather.1 = f32[1536,96]{1,0:T(8,128)S(1)} all-gather(f32[96,96]{1,0:T(8,128)S(1)} %fusion.45), channel_id=3, replica_groups=mesh['grp'=2,'row'=16] {'row'}, dimensions={0}, use_global_device_ids=true | all-gather | bytes 626688 | tf_op jit(solution)/shard_map/all_gather | solution.py:33
  310.5 0.1 reduce_sum.19
  310.5 0.1 copy.11
  310.7 0.1 copy.12
  310.8 8.8 %cholesky.55 = f32[96,96]{1,0:T(8,128)S(1)} custom-call(f32[96,96]{1,0:T(8,128)S(1)} %fusion.33), custom_call_target="Cholesky" | custom-call | tf_op jit(solution)/shard_map/jit(cholesky)/cholesky | solution.py:34
  319.6 0.6 compare_reduce_fusion
  320.2 0.7 fusion.31
  320.9 7.4 %custom-call.7 = f32[1,96,96]{1,2,0:T(8,128)S(1)} custom-call(f32[1,96,96]{2,1,0:T(8,128)S(1)} %fusion.31), custom_call_target="InvertDiagBlocksLowerTriangular" | custom-call | tf_op jit(solution)/shard_map/triangular_solve/custom-call.0 | solution.py:35
  328.2 0.3 convolution_bitcast_fusion.2
  328.5 7.5 %convolution_bitcast_fusion = f32[16384,96]{0,1:T(8,128)} fusion(bf16[256,16384]{1,0:T(8,128)(2,1)} %param.7, f32[256,96]{0,1:T(8,128)S(1)} %convolution_bitcast_fusion.2, f32[256]{0:T(256)S(1)} %bitcast.69), kind=kOutput, calls=%fused_computation | convolution fusion | flops 805355520 | bytes 14779392 | tf_op jit(solution)/shard_map/dot_general | solution.py:83
  336.1 0.0 reduce-scatter.5.cloned.1.call-update
  336.1 82.4 %reduce-scatter.5.cloned.1.call-done = f32[1024,96]{0,1:T(8,128)} async-done(((f32[16384,96]{0,1:T(8,128)}), f32[1024,96]{0,1:T(8,128)}) %reduce-scatter.5.cloned.1.call-update) | async-done | bytes 393232 | tf_op jit(solution)/shard_map/reduce_scatter | solution.py:82
  418.5 1.8 copy_bitcast_fusion
  (17 shorter events, 0.1 us)
Async XLA Ops:
  7.2 40.0 %copy-start = (f32[8]{0:T(128)S(1)}, f32[8]{0:T(128)}, u32[]{:S(2)}) copy-start(f32[8]{0:T(128)} %param.9) | copy-start | bytes 100
  7.2 10.8 %copy-start.1 = (f32[96,8,128]{2,1,0:T(8,128)S(1)}, f32[96,8,128]{2,1,0:T(8,128)}, u32[]{:S(2)}) copy-start(f32[96,8,128]{2,1,0:T(8,128)} %param.10) | copy-start | bytes 1179652
  7.2 90.5 %all-gather.5.cloned.1.call-start = ((), (), s32[]{:S(2)}) async-start(), calls=%async_computation.2 | async-start | bytes 3342336 | tf_op jit(solution)/shard_map/all_gather | solution.py:53
  8.5 3.7 collective-permute-start.1
  10.9 5.2 %collective-permute-start = (f32[96,1,128]{2,1,0:T(1,128)S(1)}, f32[96,1,128]{2,1,0:T(1,128)S(1)}, u32[]{:S(2)}, u32[]{:S(2)}) collective-permute-start(f32[96,1,128]{2,1,0:T(1,128)S(1)} %get-tuple-element.15), channel_id=1, source_target_pairs={{1,0},{2,1},{3,2},{4,3},{5,4},{6,5},{7,6},{8,7},{9,8},{10,9},{11,1... | collective-permute-start | bytes 147464 | tf_op jit(solution)/shard_map/ppermute | solution.py:18
  18.4 6.0 %collective-permute-start.3 = (f32[96,1,128]{2,1,0:T(1,128)S(1)}, f32[96,1,128]{2,1,0:T(1,128)S(1)}, u32[]{:S(2)}, u32[]{:S(2)}) collective-permute-start(f32[96,1,128]{2,1,0:T(1,128)S(1)} %get-tuple-element.12), channel_id=1, source_target_pairs={{0,1},{1,2},{2,3},{3,4},{4,5},{5,6},{6,7},{7,8},{8,9},{9,10},{10,1... | collective-permute-start | bytes 147464 | tf_op jit(solution)/shard_map/ppermute | solution.py:17
  23.1 3.1 collective-permute-start.2
  27.5 6.3 %collective-permute-start.5 = (f32[96,1,128]{2,1,0:T(1,128)S(1)}, f32[96,1,128]{2,1,0:T(1,128)S(1)}, u32[]{:S(2)}, u32[]{:S(2)}) collective-permute-start(f32[96,1,128]{2,1,0:T(1,128)S(1)} %get-tuple-element.10), channel_id=1, source_target_pairs={{0,1},{1,2},{2,3},{3,4},{4,5},{5,6},{6,7},{7,8},{8,9},{9,10},{10,1... | collective-permute-start | bytes 147464 | tf_op jit(solution)/shard_map/ppermute | solution.py:17
  32.5 3.1 collective-permute-start.4
  36.9 6.4 %collective-permute-start.7 = (f32[96,1,128]{2,1,0:T(1,128)S(1)}, f32[96,1,128]{2,1,0:T(1,128)S(1)}, u32[]{:S(2)}, u32[]{:S(2)}) collective-permute-start(f32[96,1,128]{2,1,0:T(1,128)S(1)} %get-tuple-element.8), channel_id=1, source_target_pairs={{0,1},{1,2},{2,3},{3,4},{4,5},{5,6},{6,7},{7,8},{8,9},{9,10},{10,1... | collective-permute-start | bytes 147464 | tf_op jit(solution)/shard_map/ppermute | solution.py:17
  42.0 5.1 %copy-start.3 = (s32[256]{0:T(256)S(1)}, s32[256]{0:T(256)}, u32[]{:S(2)}) copy-start(s32[256]{0:T(256)} %param.8) | copy-start | bytes 3076
  42.0 3.1 collective-permute-start.6
  47.1 187.4 %reduce-scatter.3.cloned.1.call-start = ((), (), s32[]{:S(2)}) async-start(), calls=%async_computation.3 | async-start | bytes 6684672 | tf_op jit(solution)/shard_map/reduce_scatter | solution.py:64
  152.0 129.9 %all-gather.7.cloned.1.call-start = ((), (), s32[]{:S(2)}) async-start(), calls=%async_computation.4 | async-start | bytes 3342336 | tf_op jit(solution)/shard_map/all_gather | solution.py:76
  236.2 182.3 %reduce-scatter.5.cloned.1.call-start = ((), (), s32[]{:S(2)}) async-start(), calls=%async_computation.5 | async-start | bytes 6684672 | tf_op jit(solution)/shard_map/reduce_scatter | solution.py:82
  328.5 7.5 %copy-start.2 = (f32[256,96]{0,1:T(8,128)}, f32[256,96]{0,1:T(8,128)S(1)}, u32[]{:S(2)}) copy-start(f32[256,96]{0,1:T(8,128)S(1)} %convolution_bitcast_fusion.2) | copy-start | bytes 294916
Sparse Core Ops, SparseCore 0:
  47.2 50.3 all-gather.4
  152.2 82.3 reduce-scatter.2
  237.3 44.6 all-gather.6
  336.2 82.2 reduce-scatter.4
